TPU v7x, 256 devices: a whole 4x4x8 slice. The times are simulated.
256 devices in a mesh: ctx: 16 (over x, y), head: 16 (over z, core).
Axes of the slice: x: 4, y: 4, z: 8, core: 2. Of those that a mesh axis runs over, the one named last changes fastest.
Arguments:
- tokens: bfloat16 [8192, 8192], P('ctx'), may hold values from -6 to 6
- w_zx: bfloat16 [8192, 2, 8192], P('ctx', None, 'head'), may hold values from -0.0625 to 0.0625
- zx_scale: float32 [2, 8192], P(None, 'head'), may hold values from 0.5 to 2
- w_bc: bfloat16 [8192, 8, 512], P('ctx'), may hold values from -0.0625 to 0.0625
- bc_scale: float32 [8, 512], replicated, may hold values from 0.5 to 2
- w_dt: bfloat16 [8192, 128], P('ctx', 'head'), may hold values from -0.0625 to 0.0625
- conv_x: float32 [5, 8192], P(None, 'head'), may hold values from -3 to 3
- conv_bc: float32 [5, 8, 512], replicated, may hold values from -3 to 3
- tail_x: bfloat16 [3, 8192], P(None, 'head'), may hold values from -6 to 6
- tail_bc: bfloat16 [3, 8, 512], replicated, may hold values from -6 to 6
- head_params: float32 [3, 128], P(None, 'head'), may hold values from -12 to 2, as said below
- init_state: float32 [128, 64, 256], P('head'), may hold values from -1.5 to 1.5
- norm_gain: float32 [8192], P('head'), may hold values from 0.5 to 1.5
Outputs:
- mixed: bfloat16 [8192, 8192], P('ctx', 'head')
Inputs may be any that keep to these rules, and one draw needn't show every extreme that they name: `head_params`: row 0 lies in -3.5 to -2.5 and row 2 in 0.5 to 1.5.
All inputs are finite; a program needn't handle non-finite values.
Results may differ from a plain program's by a relative error of at most 0.0052.
Values may be sent and summed in bfloat16 or wider, within the bound.
A program may use at most 256 MiB of HBM per device.

v0:
```python
import jax
import jax.numpy as jnp
from jax import lax
from jax.sharding import PartitionSpec as P

H = 128
P_SIZE = 64
N = 256
G = 8
K = 4


def passed_along(x, axis, by):
    length = lax.axis_size(axis)
    pairs = [(i, i + by) for i in range(length) if 0 <= i + by < length]
    return lax.ppermute(x, axis, pairs)


def prefix(part, axis, combine, identity):
    place = lax.axis_index(axis)
    gathered = jax.tree.map(lambda a: lax.all_gather(a, axis), part)
    state = jax.tree.map(lambda a, e: jnp.zeros_like(a) + jnp.asarray(e, a.dtype), part, identity)

    def one(lap, state):
        return combine(
            state, jax.tree.map(lambda a: lax.dynamic_index_in_dim(a, lap, 0, False), gathered)
        )

    return lax.fori_loop(0, place, one, state)


def conv_silu(values, before, taps):
    length = values.shape[0]
    padded = jnp.concatenate([before, values], 0).astype(jnp.float32)
    summed = taps[K]
    for tap_index in range(K):
        summed = summed + taps[tap_index] * padded[tap_index : tap_index + length]
    return jax.nn.silu(summed).astype(jnp.bfloat16)


def pick_group(values, group_index, axis_index):
    chosen = lax.dynamic_index_in_dim(values, group_index, axis_index, keepdims=False)
    return chosen


def body(
    tokens,
    w_zx,
    zx_scale,
    w_bc,
    bc_scale,
    w_dt,
    conv_x,
    conv_bc,
    tail_x,
    tail_bc,
    head_params,
    init_state,
    norm_gain,
):
    highest = lax.Precision.HIGHEST
    tok_rows = tokens.shape[0]
    local_heads = head_params.shape[1]
    channels = local_heads * P_SIZE
    per_group = H // G
    group_index = lax.axis_index("head") * local_heads // per_group
    bc_rows = pick_group(w_bc, group_index, 1)
    bc_scales = pick_group(bc_scale, group_index, 0)
    bc_taps = pick_group(conv_bc, group_index, 1)
    bc_tail = pick_group(tail_bc, group_index, 1)
    zx_rows = w_zx.reshape(w_zx.shape[0], 2 * channels)
    pieces = (
        lax.all_gather(zx_rows, "ctx", axis=0, tiled=True),
        lax.all_gather(bc_rows, "ctx", axis=0, tiled=True),
        lax.all_gather(w_dt, "ctx", axis=0, tiled=True),
    )
    zx_sum, bc_sum, step_sum = tuple(
        (jnp.dot(tokens, piece, preferred_element_type=jnp.float32) for piece in pieces)
    )
    zx_val = (zx_sum.reshape(tok_rows, 2, channels) * zx_scale).astype(jnp.bfloat16)
    gate = zx_val[:, 0]
    inner_in = zx_val[:, 1]
    bc_val = (bc_sum * bc_scales).astype(jnp.bfloat16)
    step_size = jax.nn.softplus(step_sum + head_params[0])
    edge = jnp.concatenate([inner_in[tok_rows - (K - 1) :], bc_val[tok_rows - (K - 1) :]], 1)
    arrived = passed_along(edge, "ctx", 1)
    previous = jnp.concatenate([tail_x, bc_tail], 1)
    arrived = jnp.where(lax.axis_index("ctx") == 0, previous, arrived)
    xconv = conv_silu(inner_in, arrived[:, :channels], conv_x)
    bconv = conv_silu(bc_val, arrived[:, channels:], bc_taps)
    b_part = bconv[:, :N]
    c_part = bconv[:, N:]
    x_heads = xconv.reshape(tok_rows, local_heads, P_SIZE).astype(jnp.float32)
    rate = -jnp.exp(head_params[1]) * step_size
    cumul = jnp.cumsum(rate, 0)
    cumul_t = cumul.T
    order = jnp.arange(tok_rows)
    lower = order[:, None] >= order[None, :]
    spread = cumul_t[:, :, None] - cumul_t[:, None, :]
    decay = jnp.where(lower[None], jnp.exp(jnp.minimum(spread, 0.0)), 0.0)
    scores = jnp.dot(c_part, b_part.T, preferred_element_type=jnp.float32)
    weights = decay * scores[None] * step_size.T[:, None, :]
    inner = jnp.einsum("hts,shp->thp", weights, x_heads, precision=highest)
    log_total = cumul[tok_rows - 1]
    fade = jnp.exp(log_total[None, :] - cumul) * step_size
    local_state = jnp.einsum(
        "sh,shp,sn->hpn", fade, x_heads, b_part.astype(jnp.float32), precision=highest
    )

    def combine(earlier, later):
        return (earlier[0] + later[0], jnp.exp(later[0])[:, None, None] * earlier[1] + later[1])

    before_log, before_state = prefix(
        (log_total, local_state),
        "ctx",
        combine,
        (jnp.zeros_like(log_total), jnp.zeros_like(local_state)),
    )
    incoming = jnp.exp(before_log)[:, None, None] * init_state + before_state
    carried = (
        jnp.einsum("tn,hpn->thp", c_part.astype(jnp.float32), incoming, precision=highest)
        * jnp.exp(cumul)[:, :, None]
    )
    y_val = inner + carried + head_params[2][None, :, None] * x_heads
    gated = y_val.reshape(tok_rows, channels) * jax.nn.silu(gate.astype(jnp.float32))
    squares = jnp.sum(gated * gated, axis=1)
    slot_hits = (jnp.arange(G) == group_index).astype(jnp.float32)
    placed = slot_hits[:, None] * squares[None, :]
    group_sums = lax.psum(placed, "head")
    totals = lax.dynamic_index_in_dim(group_sums, group_index, 0, keepdims=False)
    meansq = totals / (per_group * P_SIZE)
    mixed = gated * lax.rsqrt(meansq + 1e-05)[:, None] * norm_gain
    return mixed.astype(jnp.bfloat16)


def solution(mesh):
    return jax.shard_map(
        body,
        mesh=mesh,
        in_specs=(
            P("ctx", None),
            P("ctx", None, "head"),
            P(None, "head"),
            P("ctx", None, None),
            P(),
            P("ctx", "head"),
            P(None, "head"),
            P(),
            P(None, "head"),
            P(),
            P(None, "head"),
            P("head", None, None),
            P("head"),
        ),
        out_specs=P("ctx", "head"),
        check_vma=False,
    )
```

profile of v0, /device:TPU:30, one launch (start us, length us, event | category | flops | bytes accessed | tf_op | source)
XLA Modules:
  0.0 391.0 jit_solution(2558766528780283261)
XLA Ops:
  6.5 3.3 constant_dynamic-slice_fusion.8
  10.8 2.5 copy.40
  13.5 21.8 %all_gather.20 = bf16[8192,8]{0,1:T(8,128)(2,1)S(1)} all-gather(bf16[512,8]{0,1:T(8,128)(2,1)} %param.20), channel_id=1, replica_groups=mesh['ctx'=16,'head'=16] {'ctx'}, dimensions={0}, use_global_device_ids=true | all-gather | bytes 139264 | tf_op jit(solution)/shard_map/all_gather | solution.py:75
  36.1 5.7 %convolution_add_fusion = f32[512,8]{0,1:T(8,128)S(1)} fusion(bf16[512,8192]{1,0:T(8,128)(2,1)} %param.15, bf16[8192,8]{0,1:T(8,128)(2,1)S(1)} %all_gather.20, f32[8]{0:T(128)S(1)} %get-tuple-element.93), kind=kOutput, calls=%fused_computation.30 | convolution fusion | flops 67112960 | bytes 8536096 | tf_op jit(solution)/shard_map/dot_general | solution.py:78
  45.1 42.5 %all-gather.9.cloned.1.call-done = bf16[8192,1,512]{2,0,1:T(8,128)(2,1)} async-done(((bf16[512,1,512]{2,0,1:T(8,128)(2,1)}), bf16[8192,1,512]{2,0,1:T(8,128)(2,1)}) %all-gather.9.cloned.1.call-update) | async-done | bytes 8388624 | tf_op jit(solution)/shard_map/all_gather | solution.py:74
  87.6 10.2 %fusion.27 = bf16[512,512]{1,0:T(8,128)(2,1)S(1)} fusion(bf16[512,8192]{1,0:T(8,128)(2,1)} %param.15, bf16[8192,1,512]{2,0,1:T(8,128)(2,1)} %all-gather.9.cloned.1.call-done, f32[512]{0:T(512)S(1)} %bitcast.142), kind=kOutput, calls=%fused_computation.29 | convolution fusion | flops 4295491584 | bytes 17303552 | tf_op jit(solution)/shard_map/dot_general | solution.py:78
  98.7 107.3 %all-gather.7.cloned.1.call-done = bf16[8192,1024]{1,0:T(8,128)(2,1)} async-done(((bf16[512,1024]{1,0:T(8,128)(2,1)}), bf16[8192,1024]{1,0:T(8,128)(2,1)}) %all-gather.7.cloned.1.call-update) | async-done | bytes 16777232 | tf_op jit(solution)/shard_map/all_gather | solution.py:73
  206.0 14.3 %fusion.69 = f32[512,1024]{1,0:T(8,128)S(1)} fusion(bf16[512,8192]{1,0:T(8,128)(2,1)} %param.15, bf16[8192,1024]{1,0:T(8,128)(2,1)} %all-gather.7.cloned.1.call-done), kind=kOutput, calls=%fused_computation.115 | convolution fusion | flops 8589934592 | bytes 27262976 | tf_op jit(solution)/shard_map/dot_general | solution.py:78
  220.7 1.5 collective-permute-start
  222.4 3.9 collective-permute-done
  226.5 1.5 multiply_convert_fusion.1
  228.0 2.1 copy.31
  231.5 2.5 fusion.30
  234.0 21.3 %all-gather.2 = f32[16,1,8]{2,1,0:T(1,128)S(1)} all-gather(f32[1,1,8]{2,1,0:T(1,128)S(1)} %bitcast.141), channel_id=1, replica_groups=mesh['ctx'=16,'head'=16] {'ctx'}, dimensions={0}, use_global_device_ids=true | all-gather | bytes 544 | tf_op jit(solution)/shard_map/all_gather | solution.py:21
  255.5 1.4 copy.35
  256.9 1.4 fusion.53
  258.2 8.7 %fusion.16 = f32[512,8,64]{0,2,1:T(8,128)} fusion(bf16[512,8,64]{0,2,1:T(8,128)(2,1)} %bitcast.122, f32[8,512]{1,0:T(8,128)S(1)} %get-tuple-element.83, f32[512,512]{1,0:T(8,128)S(1)} %fusion.53, f32[8,512]{1,0:T(8,128)S(1)} %add_bitcast_fusion.1, pred[512,512]{1,0:T(8,128)(4,1)S(1)} %iota_compare_fusion), kind=kOutput, calls=%fused_computation.21 | convolution fusion | flops 1621098496 | bytes 2916352 | tf_op jit(solution)/shard_map/hts,shp->thp/dot_general | solution.py:103
  266.9 44.0 %all-gather.11.cloned.1.call-done = f32[128,64,256]{2,1,0:T(8,128)} async-done(((f32[8,64,256]{2,1,0:T(8,128)}), f32[128,64,256]{2,1,0:T(8,128)}) %all-gather.11.cloned.1.call-update) | async-done | bytes 8388624 | tf_op jit(solution)/shard_map/all_gather | solution.py:21
  311.0 18.8 %while.12 = (s32[]{:T(128)}, f32[8]{0:T(128)S(1)}, f32[8,64,256]{2,1,0:T(8,128)S(1)}, s32[]{:T(128)}, f32[16,8]{1,0:T(8,128)S(1)}, /*index=5*/f32[16,8,64,256]{3,2,1,0:T(8,128)}, s32[]{:T(128)}, s32[]{:T(128)}, s32[]{:T(128)}) while((s32[]{:T(128)}, f32[8]{0:T(128)S(1)}, f32[8,64,256]{2,1,0:T(8,128)S(1)}, s32[]{:T(128)}, ...), condition=%wide.region_3.4_spmd, body=%wide.region_2.3_spmd.sunk | while | flops 262157 | bytes 1573167 | solution.py:29
  311.1 1.2 bitcast_add_fusion.3
  313.6 1.2 bitcast_add_fusion.3
  329.9 3.6 multiply_reduce_fusion
  333.5 1.6 copy.34
  335.1 48.1 %psum.7 = f32[8,512]{1,0:T(8,128)S(1)} all-reduce(f32[8,512]{1,0:T(8,128)S(1)} %broadcast_multiply_fusion), channel_id=1, replica_groups=mesh['ctx'=16,'head'=16] {'head'}, use_global_device_ids=true, to_apply=%region_5.6 | all-reduce | flops 4096 | bytes 32768 | tf_op jit(solution)/shard_map/psum | solution.py:129
  (87 shorter events, 25.6 us)
Async XLA Ops:
  6.5 6.9 %copy-start = (bf16[3,8,512]{2,1,0:T(8,128)(2,1)S(1)}, bf16[3,8,512]{2,1,0:T(8,128)(2,1)}, u32[]{:S(2)}) copy-start(bf16[3,8,512]{2,1,0:T(8,128)(2,1)} %param.24) | copy-start | bytes 73732
  6.5 38.5 %copy-start.6 = (f32[5,512]{1,0:T(8,128)S(1)}, f32[5,512]{1,0:T(8,128)}, u32[]{:S(2)}) copy-start(f32[5,512]{1,0:T(8,128)} %param.21) | copy-start | bytes 30724
  6.5 81.1 %all-gather.9.cloned.1.call-start = ((), (), s32[]{:S(2)}) async-start(), calls=%async_computation.1 | async-start | bytes 8912896 | tf_op jit(solution)/shard_map/all_gather | solution.py:74
  10.8 195.3 %all-gather.7.cloned.1.call-start = ((), (), s32[]{:S(2)}) async-start(), calls=%async_computation | async-start | bytes 17825792 | tf_op jit(solution)/shard_map/all_gather | solution.py:73
  13.4 297.6 %all-gather.11.cloned.1.call-start = ((), (), s32[]{:S(2)}) async-start(), calls=%async_computation.2 | async-start | bytes 8912896 | tf_op jit(solution)/shard_map/all_gather | solution.py:21
  97.9 0.8 copy-start.4
  98.7 121.7 %copy-start.7 = (f32[2,512]{1,0:T(2,128)S(1)}, f32[2,512]{1,0:T(2,128)}, u32[]{:S(2)}) copy-start(f32[2,512]{1,0:T(2,128)} %param.17) | copy-start | bytes 12292
  98.7 127.6 %copy-start.8 = (bf16[3,512]{1,0:T(4,128)(2,1)S(1)}, bf16[3,512]{1,0:T(4,128)(2,1)}, u32[]{:S(2)}) copy-start(bf16[3,512]{1,0:T(4,128)(2,1)} %param.23) | copy-start | bytes 9220
  206.0 20.2 %copy-start.5 = (bf16[512,512]{1,0:T(8,128)(2,1)S(1)}, bf16[512,512]{1,0:T(8,128)(2,1)}, u32[]{:S(2)}) copy-start(bf16[512,512]{1,0:T(8,128)(2,1)} %copy-done.4) | copy-start | bytes 1572868
  220.7 5.5 %collective-permute-start = (bf16[3,1024]{1,0:T(4,128)(2,1)S(1)}, bf16[3,1024]{1,0:T(4,128)(2,1)S(1)}, u32[]{:S(2)}, u32[]{:S(2)}) collective-permute-start(bf16[3,1024]{1,0:T(4,128)(2,1)S(1)} %pad_maximum_fusion), channel_id=1, source_target_pairs={{0,16},{16,32},{32,48},{48,64},{64,80},{80,96},{96,112},{112,128},... | collective-permute-start | bytes 18440 | tf_op jit(solution)/shard_map/ppermute | solution.py:16
  230.7 0.8 copy-start.1
  258.2 71.6 %copy-start.2 = (bf16[512,512]{1,0:T(8,128)(2,1)S(1)}, bf16[512,512]{1,0:T(8,128)(2,1)}, u32[]{:S(2)}) copy-start(bf16[512,512]{1,0:T(8,128)(2,1)} %copy-done.1) | copy-start | bytes 1572868
  258.2 71.6 %copy-start.3 = (bf16[512,512]{0,1:T(8,128)(2,1)S(1)}, bf16[512,512]{0,1:T(8,128)(2,1)}, u32[]{:S(2)}) copy-start(bf16[512,512]{0,1:T(8,128)(2,1)} %copy.31) | copy-start | bytes 1572868
  311.0 72.3 %copy-start.9 = (f32[512]{0:T(512)S(1)}, f32[512]{0:T(512)}, u32[]{:S(2)}) copy-start(f32[512]{0:T(512)} %param.27) | copy-start | bytes 6148
Sparse Core Ops, SparseCore 0:
  10.9 76.6 all-gather.8
  90.1 115.9 all-gather.6
  234.2 76.7 all-gather.10
where the time goes:
time: 392 us; the launch traced here: 391 us
  waiting for transfers between devices  198 us (51%)
  blocking collectives  91.2 us (23%)
  matrix products  46.4 us (12%)
  other arithmetic  24.9 us (6%)
  local copies, waits for them, and re-layouts  15.4 us (4%)
  between operations  13.4 us (3%)
    all_gather x1, waiting for transfers between devices, body(): lax.all_gather(zx_rows, 'ctx', axis=0, tiled=True)  107 us
    psum x1, blocking collectives, body(): group_sums = lax.psum(placed, 'head')  48.1 us
    all_gather x1, waiting for transfers between devices, prefix(): gathered = jax.tree.map(lambda a: lax.all_gather(a, axis), part)  44 us
    all_gather x1, waiting for transfers between devices, body(): lax.all_gather(bc_rows, 'ctx', axis=0, tiled=True)  42.5 us
    dot_general x3, matrix products, body(): jnp.dot(tokens, piece, preferred_element_type=jnp.float32)  30.3 us
    all_gather x1, blocking collectives, body(): lax.all_gather(w_dt, 'ctx', axis=0, tiled=True)  21.8 us
    all_gather x1, blocking collectives, prefix(): gathered = jax.tree.map(lambda a: lax.all_gather(a, axis), part)  21.3 us
    add x15, other arithmetic, combine(): jnp.exp(later[0])[:, None, None] * earlier[1] + later[1]  18.1 us
  transfers between devices with their start and end apart: 4, of which 4 were waited for; matrix products, arithmetic and copies ran while one was open for 9% of the time, Pallas kernels for 0%

commit v1 on v0

v1 whole, which is shorter than its diff:
```python
import jax
import jax.numpy as jnp
from jax import lax
from jax.experimental import pallas as pl
from jax.experimental.pallas import tpu as pltpu
from jax.sharding import PartitionSpec as P

H = 128
P_SIZE = 64
N = 256
G = 8
K = 4
MESH = pl.DeviceIdType.MESH
HALO = 16
NT = (((1,), (1,)), ((), ()))
TN = (((0,), (0,)), ((), ()))
JS = (0, 1, -1, 2)
ROWS = (((0, 128, 256), (256, 384, 528)), ((0, 128, 256), (256, 384, 512)))


def kernel(tok_hbm, w1_hbm, w2_hbm, *refs):
    small_in, out, small, refs = refs[:9], refs[9], refs[10:19], refs[19:]
    zxs, bcs, convx, convbc, tailx, tailbc, hp, gain, init = small
    (
        par, tok, w1, w2, acc1, acc2, accd, wp, ext, xb, bcb, gs, yb, cum, cumt, dtt,
        st1, rc1, st2, rc2, sq,
        wsend, wrecv, as1, ar1, as2, ar2, psend, precv, hsend, hrecv, lsem, ssem,
    ) = refs
    f32, bf16 = jnp.float32, jnp.bfloat16
    me = lax.axis_index("ctx")
    hd = lax.axis_index("head")
    core = lax.rem(hd, 2)
    mate = hd + 1 - 2 * core
    mx, my = me // 4, lax.rem(me, 4)

    def at(half, da, db):
        ox = half * da + (1 - half) * db
        oy = (1 - half) * da + half * db
        return lax.rem(mx + ox + 4, 4) * 4 + lax.rem(my + oy + 4, 4)

    barrier = pltpu.get_barrier_semaphore()
    for o in range(1, 16):
        pl.semaphore_signal(
            barrier, inc=1, device_id={"ctx": lax.rem(me + o, 16)}, device_id_type=MESH
        )
    pl.semaphore_signal(barrier, inc=1, device_id={"head": mate}, device_id_type=MESH)

    tok_in = pltpu.make_async_copy(tok_hbm, tok.at[pl.ds(0, 512), :], lsem.at[0])
    w1_in = pltpu.make_async_copy(w1_hbm, w1.at[me], lsem.at[1])
    w2_in = pltpu.make_async_copy(w2_hbm, w2.at[me], lsem.at[2])
    w1_in.start()
    tok_in.start()
    w2_in.start()
    small_copies = [
        pltpu.make_async_copy(a, b, ssem.at[n]) for n, (a, b) in enumerate(zip(small_in, small))
    ]
    for c in small_copies:
        c.start()
    pl.semaphore_wait(barrier, 16)

    sent = []

    def remote(src, dst, ssem, rsem, who):
        c = pltpu.make_async_remote_copy(
            src_ref=src, dst_ref=dst, send_sem=ssem, recv_sem=rsem,
            device_id=who, device_id_type=MESH,
        )
        sent.append(c)
        return c

    made = {}

    def weight(kind, half, phase, j, d):
        key = (kind, half, phase, j, d)
        if key in made:
            return made[key]
        index = len(made)
        start, split, end = ROWS[kind][half]
        if phase in (1, 3):
            start, end = (start, split) if d == 1 else (split, end)
        da, db = ((0, 0), (-d, 0), (j, 0), (j, -d))[phase]
        origin = at(half, da, db)
        who = at(half, d, 0) if phase < 2 else at(half, 0, d)
        rows = pl.ds(start, end - start)
        buf = (w1, w2)[kind]
        src = buf.at[origin, rows, :]
        if (da, db) == (0, 0):
            src = (w1_hbm, w2_hbm)[kind].at[rows, :]
        made[key] = remote(
            src, buf.at[origin, rows, :], wsend.at[index], wrecv.at[index], {"ctx": who}
        )
        return made[key]

    hd2 = [(half, d) for half in (0, 1) for d in (1, -1)]

    def issue(kind, step):
        todo = {
            0: [(0, (0,)), (2, (0,))],
            1: [(1, (0,)), (2, (1, -1))],
            2: [(3, (0,))],
            3: [(2, (2,))],
            4: [(3, (1, -1))],
            5: [(3, (2,))],
        }[step]
        for phase, js in todo:
            for j in js:
                for half, d in hd2:
                    weight(kind, half, phase, j, d).start()

    def arrive(kind, step):
        todo = {
            1: [(0, (0,))],
            2: [(2, (0,))],
            3: [(1, (0,))],
            4: [(2, (1, -1))],
            5: [(2, (2,))],
            6: [(3, (0, 1, -1))],
            7: [(3, (2,))],
        }[step]
        for phase, js in todo:
            for j in js:
                for half, d in hd2:
                    weight(kind, half, phase, j, d).wait_recv()

    def unit1(half, origin):
        d0 = pl.multiple_of(origin * 512 + half * 256, 256)
        r0 = pl.multiple_of(half * 256, 256)
        for n in range(3):
            cs = pl.ds(n * 256, 256)
            acc1[:, cs] += jnp.dot(
                tok[:, pl.ds(d0, 256)], w1[origin, pl.ds(r0, 256), cs],
                preferred_element_type=f32,
            )

        @pl.when(half == 1)
        def _():
            wp[pl.ds(0, 16), :] = w1[origin, pl.ds(512, 16), pl.ds(0, 512)]
            accd[...] += lax.dot_general(
                tok[pl.ds(0, 512), pl.ds(pl.multiple_of(origin * 512, 512), 512)],
                wp[...], NT, preferred_element_type=f32,
            )

    def unit2(half, origin):
        d0 = pl.multiple_of(origin * 512 + half * 256, 256)
        r0 = pl.multiple_of(half * 256, 256)
        for n in range(2):
            cs = pl.ds(n * 256, 256)
            acc2[:, cs] += jnp.dot(
                tok[pl.ds(0, 512), pl.ds(d0, 256)], w2[origin, pl.ds(r0, 256), cs],
                preferred_element_type=f32,
            )

    def multiply(kind, step):
        unit = (unit1, unit2)[kind]
        count = {0: 2, 1: 4, 2: 4, 3: 2, 4: 8, 5: 4, 6: 6, 7: 2}[step]

        def one(u, carry):
            half = lax.rem(u, 2)
            v = u // 2
            sign = 1 - 2 * lax.rem(v, 2)
            sign2 = 1 - 2 * (v // 2)
            rel = {
                0: (0, 0), 1: (sign, 0), 2: (0, sign), 3: (2, 0),
                4: (sign, sign2), 5: (2, sign), 6: (v - 1, 2), 7: (2, 2),
            }[step]
            unit(half, at(half, rel[0], rel[1]))
            return carry

        lax.fori_loop(0, count, one, 0)

    issue(0, 0)
    halo = remote(
        tok_hbm.at[pl.ds(512 - HALO, HALO), :], tok.at[pl.ds(512, HALO), :],
        hsend.at[0], hrecv.at[0], {"ctx": lax.rem(me + 1, 16)},
    )
    halo.start()
    for c in small_copies:
        c.wait()
    group = hd // 2

    def side(v):
        return jnp.where(core == 0, v[:, 0:256], v[:, 256:512])

    par[...] = jnp.zeros_like(par)
    par[0:5, 0:512] = convx[...]
    par[5:6, 0:512] = zxs[1:2, :]
    par[5:6, 512:768] = side(bcs[pl.ds(group, 1), :])
    for k in range(5):
        par[k:k + 1, 512:768] = side(convbc[k, pl.ds(group, 1), :])
    par[9:10, 0:512] = gain[...]
    par[10:11, 0:512] = zxs[0:1, :]
    left1 = lax.broadcasted_iota(jnp.int32, (1, 128), 1) < 64
    for p in range(4):
        par[11:12, p * 128:p * 128 + 128] = jnp.where(
            left1, hp[2:3, 2 * p:2 * p + 1], hp[2:3, 2 * p + 1:2 * p + 2]
        )
    par[12:13, 0:8] = hp[0:1, :]
    par[13:14, 0:8] = -jnp.exp(hp[1:2, :])
    par[21:24, 0:512] = tailx[...].astype(f32)
    mine = lax.broadcasted_iota(jnp.int32, (8, 512), 0) == group
    for k in range(3):
        chosen = jnp.where(mine, tailbc[k].astype(f32), 0.0)
        par[21 + k:22 + k, 512:768] = side(jnp.sum(chosen, axis=0, keepdims=True))
    acc1[...] = jnp.zeros_like(acc1)
    acc2[...] = jnp.zeros_like(acc2)
    accd[...] = jnp.zeros_like(accd)
    wp[...] = jnp.zeros_like(wp)
    tok_in.wait()
    w1_in.wait()
    w2_in.wait()
    halo.wait_recv()
    multiply(0, 0)
    for step in range(1, 6):
        arrive(0, step)
        issue(0, step)
        multiply(0, step)
    issue(1, 0)
    arrive(0, 6)
    multiply(0, 6)
    arrive(0, 7)
    multiply(0, 7)
    arrive(1, 1)
    issue(1, 1)

    scale = par[5:6, :]
    ext[8:520, :] = (acc1[0:512, :] * scale).astype(bf16).astype(f32)
    prev = (acc1[512:528, :] * scale).astype(bf16).astype(f32)
    first = jnp.where(me == 0, 1.0, 0.0).astype(f32)
    ext[0:8, :] = jnp.where(first > 0.5, par[16:24, :], prev[8:16, :])
    for r in range(4):
        summed = jnp.broadcast_to(par[4:5, :], (128, 768))
        for k in range(K):
            summed = summed + par[k:k + 1, :] * ext[5 + k + r * 128:5 + k + r * 128 + 128, :]
        act = (summed * (1.0 / (1.0 + jnp.exp(-summed)))).astype(bf16)
        xb[pl.ds(r * 128, 128), :] = act[:, 0:512]
        bcb[core, pl.ds(r * 128, 128), :] = act[:, 512:768]
    swap = remote(bcb.at[core], bcb.at[core], psend.at[0], precv.at[0], {"head": mate})
    swap.start()

    step_size = jax.nn.softplus(accd[...] + par[12:13, 0:128])
    rate_t = (step_size * par[13:14, 0:128]).T[0:16, :]
    lane = lax.broadcasted_iota(jnp.int32, (16, 512), 1)
    run = rate_t
    for s in (1, 2, 4, 8, 16, 32, 64, 128, 256):
        run = run + jnp.where(lane >= s, pltpu.roll(run, s, 1), 0.0)
    cumt[...] = run
    dtt[...] = step_size.T[0:16, :]
    cumc = jnp.concatenate([run, jnp.zeros((112, 512), f32)], 0).T
    cum[...] = cumc
    last = cumc[511:512, :]
    fade = jnp.exp(last - cumc) * step_size
    decay = jnp.exp(last)
    lanes = lax.broadcasted_iota(jnp.int32, (512, 128), 1)

    def by_head(cols, p):
        return jnp.where(lanes < 64, cols[:, 2 * p:2 * p + 1], cols[:, 2 * p + 1:2 * p + 2])

    swap.wait_recv()
    bpart = bcb[0]
    tag = lax.broadcasted_iota(jnp.int32, (16, 256), 0)
    for p in range(4):
        xf = (xb[:, pl.ds(p * 128, 128)].astype(f32) * by_head(fade, p)).astype(bf16)
        state = lax.dot_general(xf, bpart, TN, preferred_element_type=f32).astype(bf16)
        for q in range(4):
            piece = 4 * p + q
            h = piece // 2
            value = jnp.broadcast_to(decay[:, h:h + 1], (16, 256))
            hi = value.astype(bf16).astype(f32)
            mid = (value - hi).astype(bf16).astype(f32)
            low = value - hi - mid
            st1[piece, 0:32, :] = state[q * 32:q * 32 + 32, :]
            st1[piece, 32:48, :] = jnp.where(
                tag == 0, hi, jnp.where(tag == 1, mid, jnp.where(tag == 2, low, 0.0))
            ).astype(bf16)

    def exchange(src, dst, ssem, rsem):
        made_here = []
        for o in range(1, 16):
            who = lax.rem(me + o, 16)
            made_here.append(
                remote(src.at[who], dst.at[me], ssem.at[o - 1], rsem.at[o - 1], {"ctx": who})
            )
        return made_here

    ex1 = exchange(st1, rc1, as1, ar1)
    for c in ex1:
        c.start()
    rc1[me] = st1[me]
    arrive(1, 2)
    issue(1, 2)

    cpart = bcb[1]
    gs[...] = lax.dot_general(cpart, bpart, NT, preferred_element_type=f32)

    def pair(p):
        for i in range(2):
            size = 256 * (i + 1)
            rows = pl.ds(256 * i, 256)
            xp = xb[pl.ds(0, size), pl.ds(p * 128, 128)]
            lower = (
                lax.broadcasted_iota(jnp.int32, (256, size), 0) + 256 * i
                >= lax.broadcasted_iota(jnp.int32, (256, size), 1)
            )
            parts = []
            for h in (2 * p, 2 * p + 1):
                spread = cum[rows, h:h + 1] - cumt[h:h + 1, 0:size]
                e = jnp.exp(jnp.where(lower, spread, -1e30))
                m = (gs[rows, 0:size] * e * dtt[h:h + 1, 0:size]).astype(bf16)
                parts.append(jnp.dot(m, xp, preferred_element_type=f32))
            left = lax.broadcasted_iota(jnp.int32, (256, 128), 1) < 64
            cs = pl.ds(p * 128, 128)
            skip = par[11:12, p * 128:p * 128 + 128]
            yb[rows, cs] = jnp.where(left, parts[0], parts[1]) + skip * xb[rows, cs].astype(f32)

    pair(0)
    arrive(1, 3)
    issue(1, 3)
    for step in range(4):
        multiply(1, step)
    pair(1)

    for c in ex1:
        c.wait_recv()
    state = init[pl.ds(pl.multiple_of(me * 32, 32), 32), :]
    for i in range(16):
        st2[i] = state.astype(bf16)
        if i < 15:
            got = rc1[i].astype(f32)
            factor = got[32:33, :] + got[33:34, :] + got[34:35, :]
            state = factor * state + got[0:32, :]
    ex2 = exchange(st2, rc2, as2, ar2)
    for c in ex2:
        c.start()
    rc2[me] = st2[me]
    arrive(1, 4)
    issue(1, 4)
    pair(2)
    arrive(1, 5)
    issue(1, 5)
    pair(3)
    multiply(1, 4)
    multiply(1, 5)

    for c in ex2:
        c.wait_recv()
    grow = jnp.exp(cum[...])
    for p in range(4):
        cs = pl.ds(p * 128, 128)
        incoming = rc2[4 * p:4 * p + 4].reshape(128, 256)
        carried = lax.dot_general(cpart, incoming, NT, preferred_element_type=f32)
        yb[:, cs] += carried * by_head(grow, p)

    arrive(1, 6)
    multiply(1, 6)
    arrive(1, 7)
    multiply(1, 7)
    total = jnp.zeros((512, 128), f32)
    for p in range(4):
        cs = pl.ds(p * 128, 128)
        gate = (acc2[:, cs] * par[10:11, p * 128:p * 128 + 128]).astype(bf16).astype(f32)
        gated = yb[:, cs] * (gate * (1.0 / (1.0 + jnp.exp(-gate))))
        yb[:, cs] = gated
        total = total + gated * gated
    sq[core] = total
    swap2 = remote(sq.at[core], sq.at[core], psend.at[1], precv.at[1], {"head": mate})
    swap2.start()
    swap2.wait_recv()
    ms = jnp.sum(sq[0] + sq[1], axis=1, keepdims=True) * (1.0 / 1024.0)
    inv = lax.rsqrt(ms + 1e-05)
    for p in range(4):
        cs = pl.ds(p * 128, 128)
        out[:, cs] = (yb[:, cs] * inv * par[9:10, p * 128:p * 128 + 128]).astype(bf16)
    for c in sent:
        c.wait_send()


def body(
    tokens, w_zx, zx_scale, w_bc, bc_scale, w_dt, conv_x, conv_bc, tail_x, tail_bc,
    head_params, init_state, norm_gain,
):
    f32, bf16 = jnp.float32, jnp.bfloat16
    hd = lax.axis_index("head")
    group, core = hd // 2, hd % 2

    def pick(a):
        start = (0,) * (a.ndim - 2) + (group, core * 256)
        return lax.dynamic_slice(a, start, a.shape[:-2] + (1, 256)).reshape(a.shape[:-2] + (256,))

    w1 = jnp.concatenate(
        [
            jnp.concatenate([w_zx[:, 1, :], pick(w_bc)], 1),
            jnp.pad(w_dt.T, ((0, 8), (0, 256))),
        ],
        0,
    )
    w2 = w_zx[:, 0, :]

    vmem = pl.BlockSpec(memory_space=pltpu.VMEM)
    hbm = pl.BlockSpec(memory_space=pl.ANY)
    dma = pltpu.SemaphoreType.DMA
    small = (
        zx_scale, bc_scale, conv_x, conv_bc, tail_x, tail_bc, head_params,
        norm_gain.reshape(1, 512), init_state.reshape(512, 256),
    )
    return pl.pallas_call(
        kernel,
        out_shape=jax.ShapeDtypeStruct((512, 512), bf16),
        in_specs=[hbm] * 12,
        out_specs=vmem,
        scratch_shapes=[pltpu.VMEM(a.shape, a.dtype) for a in small] + [
            pltpu.VMEM((24, 768), f32),
            pltpu.VMEM((528, 8192), bf16),
            pltpu.VMEM((16, 528, 768), bf16),
            pltpu.VMEM((16, 512, 512), bf16),
            pltpu.VMEM((528, 768), f32),
            pltpu.VMEM((512, 512), f32),
            pltpu.VMEM((512, 128), f32),
            pltpu.VMEM((128, 512), bf16),
            pltpu.VMEM((520, 768), f32),
            pltpu.VMEM((512, 512), bf16),
            pltpu.VMEM((2, 512, 256), bf16),
            pltpu.VMEM((512, 512), f32),
            pltpu.VMEM((512, 512), f32),
            pltpu.VMEM((512, 128), f32),
            pltpu.VMEM((16, 512), f32),
            pltpu.VMEM((16, 512), f32),
            pltpu.VMEM((16, 48, 256), bf16),
            pltpu.VMEM((16, 48, 256), bf16),
            pltpu.VMEM((16, 32, 256), bf16),
            pltpu.VMEM((16, 32, 256), bf16),
            pltpu.VMEM((2, 512, 128), f32),
            dma((80,)), dma((80,)),
            dma((15,)), dma((15,)), dma((15,)), dma((15,)),
            dma((2,)), dma((2,)), dma((1,)), dma((1,)), dma((3,)), dma((9,)),
        ],
        compiler_params=pltpu.CompilerParams(
            collective_id=0, has_side_effects=True, vmem_limit_bytes=60 * 1024 * 1024
        ),
    )(tokens, w1, w2, *small)


def solution(mesh):
    return jax.shard_map(
        body,
        mesh=mesh,
        in_specs=(
            P("ctx", None),
            P("ctx", None, "head"),
            P(None, "head"),
            P("ctx", None, None),
            P(),
            P("ctx", "head"),
            P(None, "head"),
            P(),
            P(None, "head"),
            P(),
            P(None, "head"),
            P("head", None, None),
            P("head"),
        ),
        out_specs=P("ctx", "head"),
        check_vma=False,
    )
```

time: 392 us -> 147 us (0.38)
  the two profiles are of different devices: /device:TPU:30 before, /device:TPU:1 now
where the time goes in v1:
time: 147 us
  Pallas kernels  139 us (95%)
  local copies, waits for them, and re-layouts  7.13 us (5%)
    pallas_call x1, Pallas kernels, body(): pl.pallas_call(kernel, out_shape=jax.ShapeDtypeStruct((512, 512), bf16),...  139 us

profile of v1, /device:TPU:1, one launch (start us, length us, event | category | flops | bytes accessed | tf_op | source)
XLA Modules:
  0.0 146.8 jit_solution(4200101726066925107)
XLA Ops:
  0.0 0.0 copy-start
  0.0 2.6 %constant_dynamic-slice_fusion = bf16[512,1,256]{2,1,0:T(2,128)(2,1)S(1)} fusion(bf16[512,8,512]{2,1,0:T(8,128)(2,1)} %param.16, s32[]{:T(128)S(6)} %select_n.18, s32[]{:T(128)S(6)} %select_n.20), kind=kLoop, calls=%fused_computation.6 | loop fusion | bytes 524296 | tf_op jit(solution)/shard_map/dynamic_slice | solution.py:387
  2.7 0.0 copy-done
  2.7 1.5 %fusion.2 = (bf16[512,1,512]{2,1,0:T(2,128)(2,1)S(1)}, bf16[512,1,512]{2,1,0:T(2,128)(2,1)S(1)}) fusion(bf16[512,2,512]{2,1,0:T(2,128)(2,1)S(1)} %copy-done), kind=kLoop, calls=%fused_computation.7 | loop fusion | bytes 2097152 | tf_op jit(solution)/shard_map/slice | solution.py:396
  4.2 0.0 copy-start.1
  4.2 1.1 copy_bitcast_fusion
  5.3 0.0 copy-done.1
  5.3 0.9 fusion.1.w1_hbm
  6.2 138.7 %shard_map.127 = bf16[512,512]{1,0:T(8,128)(2,1)} custom-call(bf16[512,8192]{1,0:T(8,128)(2,1)} %tok_hbm.1, bf16[528,768]{1,0:T(8,128)(2,1)} %fusion.1.w1_hbm, bf16[512,512]{1,0:T(8,128)(2,1)} %get-tuple-element.7.w2_hbm, f32[2,512]{1,0:T(2,128)} %refs_0_.1, f32[8,512]{1,0:T(8,128)} %refs_1_.1, f32[5,512]{1,0:T(8,128)} %refs_2_.1, f32[5,8,512]{2,1,0:T(8,128)} %refs_3_.1, ...), custom_call_target="tpu_custom_call" | custom-call | tf_op jit(solution)/shard_map/pallas_call | solution.py:405
  144.9 1.9 %copy.27 = bf16[512,512]{1,0:T(8,128)(2,1)} copy(bf16[512,512]{1,0:T(8,128)(2,1)} %shard_map.127) | data formatting | bytes 1048576
  (1 shorter events, 0.0 us)
Async XLA Ops:
  0.0 2.7 %copy-start = (bf16[512,2,512]{2,1,0:T(2,128)(2,1)S(1)}, bf16[512,2,512]{2,1,0:T(2,128)(2,1)}, u32[]{:S(2)}) copy-start(bf16[512,2,512]{2,1,0:T(2,128)(2,1)} %param.14) | copy-start | bytes 3145732
  4.2 1.1 copy-start.1
